TPU v7x, 256 devices: a whole 4x4x8 slice. The times are simulated.
256 devices in a mesh: wide: 32 (over x_lo, z, core), rows: 8 (over y, x_hi).
Axes of the slice: x: 4 (x_hi: 2, x_lo: 2; x = x_hi * 2 + x_lo), y: 4, z: 8, core: 2. Of those that a mesh axis runs over, the one named last changes fastest.
Arguments:
- matrix: float32 [8192, 16384], P('rows', 'wide'), may hold values from -600 to 600, as said below
- pairing: int32 [2, 512], replicated, may hold values from 0 to 511, each once within a row
Outputs:
- rotated: float32 [8192, 16384], P('rows', 'wide')
Inputs may be any that keep to these rules, and one draw needn't show every extreme that they name: `matrix`: finite entries.
All inputs are finite; a program needn't handle non-finite values.
Results may differ from a plain program's by a relative error of at most 0.0001.
Values sent between devices are 32-bit elements; how exact they have to be, the bound alone decides.
A program may use at most 64 MiB of HBM per device.

v0:
```python
import jax
import jax.numpy as jnp
from jax import lax
from jax.sharding import PartitionSpec as P

NS_STEPS = 3
EPSILON = 1e-06
HIGH = lax.Precision.HIGHEST


def from_behind(value, axis, steps):
    count = lax.axis_size(axis)
    pairs = [(source, (source + steps) % count) for source in range(count)]
    return lax.ppermute(value, axis, pairs)


def generator(coupling, largest):
    half_cols = coupling.shape[0]
    identity = jnp.eye(half_cols, dtype=jnp.float32)
    top = jnp.concatenate([identity, coupling], axis=1)
    bottom = jnp.concatenate([-coupling.T, identity], axis=1)
    return jnp.concatenate([top, bottom], axis=0) * lax.rsqrt(1.0 + largest)


def shards(matrix, pairing):
    half_cols = matrix.shape[1] // 2
    current = matrix
    for round_index in range(pairing.shape[0]):
        columns = jnp.take(current, pairing[round_index], axis=1)
        partial_value = jnp.einsum(
            "ra,rb->ab", columns, columns, precision=HIGH, preferred_element_type=jnp.float32
        )
        gram = lax.psum(partial_value, "rows")
        norms = jnp.diagonal(gram)
        cross = gram[:half_cols, half_cols:]
        inverse = lax.rsqrt(norms + EPSILON)
        coupling = cross * inverse[:half_cols, None] * inverse[None, half_cols:]
        largest = lax.pmax(jnp.sum(coupling * coupling), "wide")
        rotation = generator(coupling, largest)
        for sweep in range(NS_STEPS):
            square = jnp.einsum(
                "ca,cb->ab", rotation, rotation, precision=HIGH, preferred_element_type=jnp.float32
            )
            rotation = 1.5 * rotation - 0.5 * jnp.dot(
                rotation, square, precision=HIGH, preferred_element_type=jnp.float32
            )
        product = jnp.dot(columns, rotation, precision=HIGH, preferred_element_type=jnp.float32)
        kept_block = product[:, :half_cols]
        moved_block = from_behind(product[:, half_cols:], "wide", 1)
        current = jnp.concatenate([kept_block, moved_block], axis=1)
    return current


def solution(mesh):
    in_specs = (P("rows", "wide"), P())
    out_specs = P("rows", "wide")
    return jax.shard_map(shards, mesh=mesh, in_specs=in_specs, out_specs=out_specs, check_vma=False)
```

profile of v0, /device:TPU:2, one launch (start us, length us, event | category | flops | bytes accessed | tf_op | source)
XLA Modules:
  0.0 418.8 jit_solution(11703738386899458625)
XLA Ops:
  7.3 1.9 copy.12
  9.3 2.7 gather_fusion.2
  11.9 7.0 %fusion.6 = f32[512,512]{1,0:T(8,128)} fusion(f32[512,1024]{1,0:T(8,128)} %gather_fusion.2, pred[512]{0:T(512)(128)(4,1)S(1)} %compare_and_fusion.1), kind=kOutput, calls=%fused_computation.12 | convolution fusion | flops 3221749760 | bytes 3146240 | tf_op jit(solution)/shard_map/ra,rb->ab/dot_general | solution.py:30
  19.0 97.5 %all-reduce.3.cloned.1.call-done = f32[512,512]{1,0:T(8,128)} async-done(((f32[512,512]{1,0:T(8,128)}), f32[512,512]{1,0:T(8,128)}) %all-reduce.3.cloned.1.call-update) | async-done | bytes 1048592 | tf_op jit(solution)/shard_map/psum | solution.py:33
  116.5 8.4 %gather_fusion = f32[512]{0:T(512)S(1)} fusion(f32[512,512]{1,0:T(8,128)} %all-reduce.3.cloned.1.call-done, s32[512]{0:T(512)S(1)} %bitcast.37), kind=kCustom, calls=%fused_computation.2 | custom fusion | bytes 8192 | tf_op jit(solution)/shard_map/jit(diagonal)/cond/branch_0_fun/gather | solution.py:34
  126.9 54.2 %pmax.14 = f32[]{:T(128)} all-reduce(f32[]{:T(128)} %get-tuple-element.8), channel_id=1, replica_groups=mesh['wide'=32,'rows'=8] {'wide'}, use_global_device_ids=true, to_apply=%region_2.4 | all-reduce | flops 1 | bytes 8 | tf_op jit(solution)/shard_map/pmax | solution.py:38
  181.9 1.9 fusion.33
  183.8 2.0 fusion.17
  185.8 1.9 fusion.58
  187.6 2.0 fusion.16
  191.5 1.9 fusion.15
  193.4 4.0 fusion.4
  198.1 16.0 %collective-permute-done = f32[1024,256]{0,1:T(8,128)S(1)} collective-permute-done((f32[1024,256]{0,1:T(8,128)S(1)}, f32[1024,256]{0,1:T(8,128)S(1)}, u32[]{:S(2)}, u32[]{:S(2)}) %collective-permute-start) | collective-permute-done | bytes 1048608 | tf_op jit(solution)/shard_map/ppermute | solution.py:14
  214.3 2.7 gather_fusion.3
  216.9 7.0 %fusion.2 = f32[512,512]{0,1:T(8,128)} fusion(f32[512,1024]{1,0:T(8,128)} %gather_fusion.3, pred[512]{0:T(512)(128)(4,1)S(1)} %compare_and_fusion), kind=kOutput, calls=%fused_computation.8 | convolution fusion | flops 3221749760 | bytes 3146240 | tf_op jit(solution)/shard_map/ra,rb->ab/dot_general | solution.py:30
  224.0 88.2 %all-reduce.5.cloned.1.call-done = f32[512,512]{0,1:T(8,128)} async-done(((f32[512,512]{0,1:T(8,128)}), f32[512,512]{0,1:T(8,128)}) %all-reduce.5.cloned.1.call-update) | async-done | bytes 1048592 | tf_op jit(solution)/shard_map/psum | solution.py:33
  312.2 8.4 %gather_fusion.1 = f32[512]{0:T(512)S(1)} fusion(f32[512,512]{0,1:T(8,128)} %all-reduce.5.cloned.1.call-done, s32[512]{0:T(512)S(1)} %bitcast.38), kind=kCustom, calls=%fused_computation.3 | custom fusion | bytes 8192 | tf_op jit(solution)/shard_map/jit(diagonal)/cond/branch_0_fun/gather | solution.py:34
  322.6 54.2 %pmax.15 = f32[]{:T(128)} all-reduce(f32[]{:T(128)} %get-tuple-element.6), channel_id=1, replica_groups=mesh['wide'=32,'rows'=8] {'wide'}, use_global_device_ids=true, to_apply=%region_5.7 | all-reduce | flops 1 | bytes 8 | tf_op jit(solution)/shard_map/pmax | solution.py:38
  377.5 1.9 fusion.30
  379.4 2.0 fusion.14
  383.3 2.0 fusion.13
  387.1 1.9 fusion.12
  389.1 4.1 fusion
  393.8 16.0 %collective-permute-done.1 = f32[1024,256]{0,1:T(8,128)S(1)} collective-permute-done((f32[1024,256]{0,1:T(8,128)S(1)}, f32[1024,256]{0,1:T(8,128)S(1)}, u32[]{:S(2)}, u32[]{:S(2)}) %collective-permute-start.1) | collective-permute-done | bytes 1048608 | tf_op jit(solution)/shard_map/ppermute | solution.py:14
  (37 shorter events, 13.8 us)
Async XLA Ops:
  6.5 110.0 %all-reduce.3.cloned.1.call-start = ((), (), s32[]{:S(2)}) async-start(), calls=%async_computation | async-start | bytes 2097152 | tf_op jit(solution)/shard_map/psum | solution.py:33
  18.9 293.3 %all-reduce.5.cloned.1.call-start = ((), (), s32[]{:S(2)}) async-start(), calls=%async_computation.1 | async-start | bytes 2097152 | tf_op jit(solution)/shard_map/psum | solution.py:33
  191.5 1.9 copy-start
  197.6 16.4 %collective-permute-start = (f32[1024,256]{0,1:T(8,128)S(1)}, f32[1024,256]{0,1:T(8,128)S(1)}, u32[]{:S(2)}, u32[]{:S(2)}) collective-permute-start(f32[1024,256]{0,1:T(8,128)S(1)} %get-tuple-element.13), channel_id=1, source_target_pairs={{0,8},{8,16},{16,24},{24,32},{32,40},{40,48},{48,56},{56,64},{64,7... | collective-permute-start | bytes 3145736 | tf_op jit(solution)/shard_map/ppermute | solution.py:14
  387.1 1.9 copy-start.1
  393.3 16.4 %collective-permute-start.1 = (f32[1024,256]{0,1:T(8,128)S(1)}, f32[1024,256]{0,1:T(8,128)S(1)}, u32[]{:S(2)}, u32[]{:S(2)}) collective-permute-start(f32[1024,256]{0,1:T(8,128)S(1)} %get-tuple-element.11), channel_id=1, source_target_pairs={{0,8},{8,16},{16,24},{24,32},{32,40},{40,48},{48,56},{56,64},{64,7... | collective-permute-start | bytes 3145736 | tf_op jit(solution)/shard_map/ppermute | solution.py:14
Sparse Core Ops, SparseCore 0:
  19.0 97.4 all-reduce.2
  224.1 88.0 all-reduce.4
where the time goes:
time: 424 us; the launch traced here: 419 us
  waiting for transfers between devices  218 us (51%)
  blocking collectives  108 us (25%)
  matrix products  45.1 us (11%)
  local copies, waits for them, and re-layouts  27.3 us (6%)
  between operations  15.4 us (4%)
    psum x2, waiting for transfers between devices, shards(): gram = lax.psum(partial_value, 'rows')  186 us
    pmax x2, blocking collectives, shards(): largest = lax.pmax(jnp.sum(coupling * coupling), 'wide')  108 us
    ppermute x2, waiting for transfers between devices, from_behind(): return lax.ppermute(value, axis, pairs)  32 us
    gather x2, local copies, waits for them, and re-layouts, shards(): norms = jnp.diagonal(gram)  16.8 us
    dot_general x2, matrix products, shards(): jnp.einsum('ra,rb->ab', columns, columns, precision=HIGH, preferred_eleme...  14 us
    dot_general x6, matrix products, shards(): jnp.dot(rotation, square, precision=HIGH, preferred_element_type=jnp.floa...  11.7 us
    dot_general x6, matrix products, shards(): jnp.einsum('ca,cb->ab', rotation, rotation, precision=HIGH, preferred_ele...  11.2 us
  transfers between devices with their start and end apart: 4, of which 4 were waited for; matrix products, arithmetic and copies ran while one was open for 0% of the time, Pallas kernels for 0%

commit v1 on v0

--- a/solution.py
+++ b/solution.py
@@ -30,7 +30,7 @@
         partial_value = jnp.einsum(
             "ra,rb->ab", columns, columns, precision=HIGH, preferred_element_type=jnp.float32
         )
-        gram = lax.psum(partial_value, "rows")
+        gram = jnp.sum(lax.all_gather(partial_value, "rows"), axis=0)
         norms = jnp.diagonal(gram)
         cross = gram[:half_cols, half_cols:]
         inverse = lax.rsqrt(norms + EPSILON)

time: 424 us -> 462 us (1.090)
  waiting for transfers between devices: 218 us -> 252 us
  local copies, waits for them, and re-layouts: 27.3 us -> 19.6 us
  other arithmetic: 4.03 us -> 11.2 us
  blocking collectives: 108 us -> 113 us
    all_gather x0 -> x2, waiting for transfers between devices: none -> 219 us  [shards(): gram = jnp.sum(lax.all_gather(partial_value, 'rows'), axis=0)]
    psum x2 -> x0, waiting for transfers between devices: 186 us -> none  [shards(): gram = lax.psum(partial_value, 'rows')]
    reduce_sum x0 -> x2, other arithmetic: none -> 9.06 us  [shards(): gram = jnp.sum(lax.all_gather(partial_value, 'rows'), axis=0)]
    gather x2, local copies, waits for them, and re-layouts: 16.8 us -> 9.05 us  [shards(): norms = jnp.diagonal(gram)]
    pmax x2, blocking collectives: 108 us -> 113 us  [shards(): largest = lax.pmax(jnp.sum(coupling * coupling), 'wide')]
where the time goes in v1:
time: 462 us; the launch traced here: 456 us
  waiting for transfers between devices  252 us (55%)
  blocking collectives  113 us (24%)
  matrix products  44.9 us (10%)
  local copies, waits for them, and re-layouts  19.6 us (4%)
  between operations  15.2 us (3%)
  other arithmetic  11.2 us (2%)
    all_gather x2, waiting for transfers between devices, shards(): gram = jnp.sum(lax.all_gather(partial_value, 'rows'), axis=0)  219 us
    pmax x2, blocking collectives, shards(): largest = lax.pmax(jnp.sum(coupling * coupling), 'wide')  113 us
    ppermute x2, waiting for transfers between devices, from_behind(): return lax.ppermute(value, axis, pairs)  32.6 us
    dot_general x2, matrix products, shards(): jnp.einsum('ra,rb->ab', columns, columns, precision=HIGH, preferred_eleme...  14 us
    dot_general x6, matrix products, shards(): jnp.dot(rotation, square, precision=HIGH, preferred_element_type=jnp.floa...  11.5 us
    dot_general x6, matrix products, shards(): jnp.einsum('ca,cb->ab', rotation, rotation, precision=HIGH, preferred_ele...  11.3 us
  transfers between devices with their start and end apart: 4, of which 4 were waited for; matrix products, arithmetic and copies ran while one was open for 0% of the time, Pallas kernels for 0%

profile of v1, /device:TPU:2, one launch (start us, length us, event | category | flops | bytes accessed | tf_op | source)
XLA Modules:
  0.0 456.5 jit_solution(7879933212775961676)
XLA Ops:
  7.3 1.9 copy.7
  9.3 2.7 gather_fusion.2
  11.9 7.0 %fusion.6 = f32[512,512]{1,0:T(8,128)} fusion(f32[512,1024]{1,0:T(8,128)} %gather_fusion.2, pred[512]{0:T(512)(128)(4,1)S(1)} %compare_and_fusion.1), kind=kOutput, calls=%fused_computation.12 | convolution fusion | flops 3221749760 | bytes 3146240 | tf_op jit(solution)/shard_map/ra,rb->ab/dot_general | solution.py:30
  19.1 114.2 %all-gather.5.cloned.1.call-done = f32[4096,512]{1,0:T(8,128)} async-done(((f32[512,512]{1,0:T(8,128)}), f32[4096,512]{1,0:T(8,128)}) %all-gather.5.cloned.1.call-update) | async-done | bytes 8388624 | tf_op jit(solution)/shard_map/all_gather | solution.py:33
  133.3 4.5 reduce_sum.36
  137.8 4.5 gather_fusion
  143.4 56.7 %pmax.14 = f32[]{:T(128)} all-reduce(f32[]{:T(128)} %get-tuple-element.8), channel_id=1, replica_groups=mesh['wide'=32,'rows'=8] {'wide'}, use_global_device_ids=true, to_apply=%region_2.4 | all-reduce | flops 1 | bytes 8 | tf_op jit(solution)/shard_map/pmax | solution.py:38
  202.6 2.0 fusion.17
  204.5 1.9 fusion.58
  206.5 1.9 fusion.16
  210.3 1.9 fusion.15
  212.2 4.0 fusion.4
  216.6 16.3 %collective-permute-done = f32[1024,256]{0,1:T(8,128)S(1)} collective-permute-done((f32[1024,256]{0,1:T(8,128)S(1)}, f32[1024,256]{0,1:T(8,128)S(1)}, u32[]{:S(2)}, u32[]{:S(2)}) %collective-permute-start) | collective-permute-done | bytes 1048608 | tf_op jit(solution)/shard_map/ppermute | solution.py:14
  233.0 2.7 gather_fusion.3
  235.7 7.0 %fusion.2 = f32[512,512]{1,0:T(8,128)} fusion(f32[512,1024]{1,0:T(8,128)} %gather_fusion.3, pred[512]{0:T(512)(128)(4,1)S(1)} %compare_and_fusion), kind=kOutput, calls=%fused_computation.8 | convolution fusion | flops 3221749760 | bytes 3146240 | tf_op jit(solution)/shard_map/ra,rb->ab/dot_general | solution.py:30
  242.7 105.0 %all-gather.7.cloned.1.call-done = f32[4096,512]{1,0:T(8,128)} async-done(((f32[512,512]{1,0:T(8,128)}), f32[4096,512]{1,0:T(8,128)}) %all-gather.7.cloned.1.call-update) | async-done | bytes 8388624 | tf_op jit(solution)/shard_map/all_gather | solution.py:33
  347.8 4.5 reduce_sum.38
  352.3 4.5 gather_fusion.1
  357.8 56.7 %pmax.15 = f32[]{:T(128)} all-reduce(f32[]{:T(128)} %get-tuple-element.6), channel_id=1, replica_groups=mesh['wide'=32,'rows'=8] {'wide'}, use_global_device_ids=true, to_apply=%region_5.7 | all-reduce | flops 1 | bytes 8 | tf_op jit(solution)/shard_map/pmax | solution.py:38
  417.0 2.0 fusion.14
  419.0 1.9 fusion.60
  420.9 1.9 fusion.13
  426.6 4.1 fusion
  431.1 16.3 %collective-permute-done.1 = f32[1024,256]{0,1:T(8,128)S(1)} collective-permute-done((f32[1024,256]{0,1:T(8,128)S(1)}, f32[1024,256]{0,1:T(8,128)S(1)}, u32[]{:S(2)}, u32[]{:S(2)}) %collective-permute-start.1) | collective-permute-done | bytes 1048608 | tf_op jit(solution)/shard_map/ppermute | solution.py:14
  (39 shorter events, 15.1 us)
Async XLA Ops:
  6.5 126.8 %all-gather.5.cloned.1.call-start = ((), (), s32[]{:S(2)}) async-start(), calls=%async_computation | async-start | bytes 9437184 | tf_op jit(solution)/shard_map/all_gather | solution.py:33
  19.0 328.8 %all-gather.7.cloned.1.call-start = ((), (), s32[]{:S(2)}) async-start(), calls=%async_computation.1 | async-start | bytes 9437184 | tf_op jit(solution)/shard_map/all_gather | solution.py:33
  210.2 1.9 copy-start
  216.4 16.4 %collective-permute-start = (f32[1024,256]{0,1:T(8,128)S(1)}, f32[1024,256]{0,1:T(8,128)S(1)}, u32[]{:S(2)}, u32[]{:S(2)}) collective-permute-start(f32[1024,256]{0,1:T(8,128)S(1)} %get-tuple-element.13), channel_id=1, source_target_pairs={{0,8},{8,16},{16,24},{24,32},{32,40},{40,48},{48,56},{56,64},{64,7... | collective-permute-start | bytes 3145736 | tf_op jit(solution)/shard_map/ppermute | solution.py:14
  424.7 1.9 copy-start.1
  431.0 16.4 %collective-permute-start.1 = (f32[1024,256]{0,1:T(8,128)S(1)}, f32[1024,256]{0,1:T(8,128)S(1)}, u32[]{:S(2)}, u32[]{:S(2)}) collective-permute-start(f32[1024,256]{0,1:T(8,128)S(1)} %get-tuple-element.11), channel_id=1, source_target_pairs={{0,8},{8,16},{16,24},{24,32},{32,40},{40,48},{48,56},{56,64},{64,7... | collective-permute-start | bytes 3145736 | tf_op jit(solution)/shard_map/ppermute | solution.py:14
Sparse Core Ops, SparseCore 0:
  19.1 114.1 all-gather.4
  242.8 104.8 all-gather.6
